TPU v7x, 32 devices: a whole 2x2x4 slice. The times are simulated.
32 devices in a mesh: gx: 4 (over y, core), gy: 8 (over z, x).
Axes of the slice: x: 2, y: 2, z: 4, core: 2. Of those that a mesh axis runs over, the one named last changes fastest.
Arguments:
- points: bfloat16 [32768, 64], P(('gx', 'gy')), may hold values from -25 to 25
- solution: float32 [32768, 32], P(('gx', 'gy')), may hold values from -6 to 6
- residual: float32 [32768, 32], P(('gx', 'gy')), may hold values from -36 to 36
- near_leaves: int32 [64, 4], P(('gx', 'gy')), may hold values from 0 to 63, as said below
- node_skeleton: int32 [32, 128], P(('gx', 'gy')), may hold values from 0 to 1023, as said below
- upper_skeleton: int32 [31, 128], replicated, may hold values from 0 to 255, as said below
- far_nodes: int32 [64, 16], P(('gx', 'gy')), may hold values from 0 to 62, as said below
Outputs:
- solution_next: float32 [32768, 32], P(('gx', 'gy'))
- residual_next: float32 [32768, 32], P(('gx', 'gy'))
- matvec_image: float32 [32768, 32], P(('gx', 'gy'))
Inputs may be any that keep to these rules, and one draw needn't show every extreme that they name: `near_leaves`: leaves are numbered in point order, 2 to a device in the flat device order. A leaf's 4 near leaves are distinct and lie on other devices of its gx row; the near leaves named by one device's leaves are all distinct, at most 2 of them lie on any one other device, and exactly 2 on some. `node_skeleton`: each row holds 128 distinct positions among its device's 1024 points. `upper_skeleton`: row u holds 128 distinct positions among the 256 skeleton points of nodes 2u+1 and 2u+2, those of 2u+1 first. `far_nodes`: each row holds 16 distinct tree nodes.
All inputs are finite; a program needn't handle non-finite values.
Results may differ from a plain program's by a relative error of at most 0.0033.
Values may be sent and summed in bfloat16 or wider, within the bound.
No kernel may reach another device: no remote copies, remote signals or barrier semaphores. Data moves between devices by JAX's collectives and lax.ppermute only.
A program may use at most 128 MiB of HBM per device.

v0:
```python
import math
import jax
import jax.numpy as jnp
from jax import lax
from jax.sharding import PartitionSpec as P

D = 64
NRHS = 32
LEAF = 512
RANK = 128
NEAR = 4
FAR = 16
LEAF_DEV = 2
LAMBDA_RIDGE = 1.0
FULL_PRECISION = lax.Precision.HIGHEST


def kernel_tile(left_points, right_points):
    left_square = jnp.sum(jnp.square(left_points.astype(jnp.float32)), axis=-1)
    right_square = jnp.sum(jnp.square(right_points.astype(jnp.float32)), axis=-1)
    cross_term = jnp.dot(left_points, right_points.T, preferred_element_type=jnp.float32)
    distance = left_square[:, None] + right_square[None, :] - 2.0 * cross_term
    return jnp.exp(distance * (-0.5 / left_points.shape[-1]))


def kernel_batch(left_points, right_points):
    left_wide = left_points.astype(jnp.float32)
    right_wide = right_points.astype(jnp.float32)
    left_square = jnp.sum(left_wide * left_wide, axis=-1)
    right_square = jnp.sum(right_wide * right_wide, axis=-1)
    cross_term = jnp.einsum("bmd,bnd->bmn", left_wide, right_wide, precision=FULL_PRECISION)
    distance = left_square[:, :, None] + right_square[:, None, :] - 2.0 * cross_term
    return jnp.exp(distance * (-0.5 / left_points.shape[-1]))


def far_kernel(own_points, far_points):
    own_square = jnp.sum(jnp.square(own_points.astype(jnp.float32)), axis=-1)
    far_square = jnp.sum(jnp.square(far_points.astype(jnp.float32)), axis=-1)
    cross_term = jnp.einsum(
        "id,frd->fir", own_points, far_points, preferred_element_type=jnp.float32
    )
    distance = own_square[None, :, None] + far_square[:, None, :] - 2.0 * cross_term
    return jnp.exp(distance * (-0.5 / own_points.shape[-1]))


def cholesky_solve(matrix, right_side):
    order = matrix.shape[0]
    indices = jnp.arange(order, dtype=jnp.int32)

    def unit(column):
        return (indices == column).astype(matrix.dtype)

    def factor_step(column, lower):
        pick = unit(column)
        matrix_column = jnp.dot(matrix, pick, precision=FULL_PRECISION)
        lower_row = jnp.dot(pick, lower, precision=FULL_PRECISION)
        remainder = matrix_column - jnp.dot(lower, lower_row, precision=FULL_PRECISION)
        pivot = jnp.sqrt(jnp.sum(remainder * pick))
        new_column = jnp.where(indices >= column, remainder / pivot, jnp.zeros_like(remainder))
        return lower + new_column[:, None] * pick[None, :]

    lower = lax.fori_loop(0, order, factor_step, jnp.zeros_like(matrix))
    diagonal_part = jnp.sum(lower * jnp.eye(order, dtype=matrix.dtype), axis=1)

    def forward_step(column, partial_value):
        pick = unit(column)
        lower_row = jnp.dot(pick, lower, precision=FULL_PRECISION)
        value = (
            jnp.dot(pick, right_side, precision=FULL_PRECISION)
            - jnp.dot(lower_row, partial_value, precision=FULL_PRECISION)
        ) / jnp.sum(diagonal_part * pick)
        return partial_value + pick[:, None] * value[None, :]

    half_solve = lax.fori_loop(0, order, forward_step, jnp.zeros_like(right_side))

    def backward_step(count, partial_value):
        column = order - 1 - count
        pick = unit(column)
        lower_column = jnp.dot(lower, pick, precision=FULL_PRECISION)
        value = (
            jnp.dot(pick, half_solve, precision=FULL_PRECISION)
            - jnp.dot(lower_column, partial_value, precision=FULL_PRECISION)
        ) / jnp.sum(diagonal_part * pick)
        return partial_value + pick[:, None] * value[None, :]

    return lax.fori_loop(0, order, backward_step, jnp.zeros_like(right_side))


def build_levels(level_points, level_weights, upper_skeleton, level_top, level_stop, block_index):
    point_levels = [level_points]
    weight_levels = [level_weights]
    for level_now in range(level_top - 1, level_stop - 1, -1):
        half_count = level_points.shape[0] // 2
        child_points = level_points.reshape(
            half_count, 2 * level_points.shape[1], level_points.shape[2]
        )
        child_weights = level_weights.reshape(
            half_count, 2 * level_weights.shape[1], level_weights.shape[2]
        )
        pick_rows = lax.dynamic_slice_in_dim(
            upper_skeleton, 2**level_now - 1 + block_index * half_count, half_count, 0
        )
        level_points = jax.vmap(
            lambda group_points, group_picks: jnp.take(group_points, group_picks, axis=0)
        )(child_points, pick_rows)
        transfer = kernel_batch(level_points, child_points)
        level_weights = (
            jnp.einsum("bmn,bnc->bmc", transfer, child_weights, precision=FULL_PRECISION)
            / jnp.sum(transfer, axis=2)[:, :, None]
        )
        point_levels.insert(0, level_points)
        weight_levels.insert(0, level_weights)
    return (point_levels, weight_levels)


def split_levels(gathered, group_total):
    per_group = gathered.reshape(group_total, -1, gathered.shape[1], gathered.shape[2])
    pieces_out = []
    width_now = 1
    offset = 0
    while offset < per_group.shape[1]:
        pieces_out.append(
            per_group[:, offset : offset + width_now].reshape(
                group_total * width_now, gathered.shape[1], gathered.shape[2]
            )
        )
        offset = offset + width_now
        width_now = width_now * 2
    return pieces_out


def leaf_image(inputs):
    own_points, near_points, near_values, far_points, far_weights = inputs
    near_tiles = jax.vmap(lambda other_points: kernel_tile(own_points, other_points))(
        near_points
    ).astype(jnp.bfloat16)
    near_part = jnp.einsum(
        "nij,njc->ic", near_tiles, near_values, preferred_element_type=jnp.float32
    )
    far_tiles = far_kernel(own_points, far_points)
    far_part = jnp.einsum("fir,frc->ic", far_tiles, far_weights, precision=FULL_PRECISION)
    return near_part / math.sqrt(own_points.shape[0]) + far_part / far_points.shape[1]


def shards(points, solution, residual, near_leaves, node_skeleton, upper_skeleton, far_nodes):
    gx_count = lax.axis_size("gx")
    gy_count = lax.axis_size("gy")
    row_index = lax.axis_index("gx")
    values_half = residual.astype(jnp.bfloat16)
    flat_points = points.reshape(LEAF_DEV, LEAF * D)
    flat_values = values_half.reshape(LEAF_DEV, LEAF * NRHS)
    request_total = LEAF_DEV * NEAR
    wanted_leaves = near_leaves.reshape(request_total) - row_index * (gy_count * LEAF_DEV)
    piece_points = lax.all_gather(flat_points, "gy", axis=0, tiled=True)
    piece_values = lax.all_gather(flat_values, "gy", axis=0, tiled=True)
    positions = jnp.arange(piece_points.shape[0], dtype=jnp.int32)
    onehot = (wanted_leaves[:, None] == positions[None, :]).astype(jnp.bfloat16)
    got_points = jnp.dot(onehot, piece_points, preferred_element_type=jnp.float32)
    got_values = jnp.dot(onehot, piece_values, preferred_element_type=jnp.float32)
    fetched_points = got_points.astype(jnp.bfloat16)
    fetched_values = got_values.astype(jnp.bfloat16)
    own_points = points.reshape(LEAF_DEV, LEAF, D)
    near_points = jnp.concatenate(
        [own_points[:, None], fetched_points.reshape(LEAF_DEV, NEAR, LEAF, D)], axis=1
    )
    near_values = jnp.concatenate(
        [
            values_half.reshape(LEAF_DEV, 1, LEAF, NRHS),
            fetched_values.reshape(LEAF_DEV, NEAR, LEAF, NRHS),
        ],
        axis=1,
    )
    skeleton_points = jnp.take(points, node_skeleton[0], axis=0)
    node_weights = jnp.dot(
        kernel_tile(skeleton_points, points), residual, precision=FULL_PRECISION
    ) / math.sqrt(points.shape[0])
    depth_total = (gx_count * gy_count).bit_length() - 1
    row_depth = gx_count.bit_length() - 1
    row_points = lax.all_gather(skeleton_points[None], "gy", axis=0, tiled=True)
    row_weights = lax.all_gather(node_weights[None], "gy", axis=0, tiled=True)
    lower_points, lower_weights = build_levels(
        row_points, row_weights, upper_skeleton, depth_total, row_depth, row_index
    )
    every_points = lax.all_gather(jnp.concatenate(lower_points, axis=0), "gx", axis=0, tiled=True)
    every_weights = lax.all_gather(
        jnp.concatenate(lower_weights, axis=0).astype(jnp.bfloat16), "gx", axis=0, tiled=True
    ).astype(jnp.float32)
    middle_points = split_levels(every_points, gx_count)
    middle_weights = split_levels(every_weights, gx_count)
    top_points, top_weights = build_levels(
        middle_points[0], middle_weights[0], upper_skeleton, row_depth, 0, 0
    )
    point_levels = top_points[:-1] + middle_points
    weight_levels = top_weights[:-1] + middle_weights
    tree_points = jnp.concatenate(point_levels, axis=0)
    tree_weights = jnp.concatenate(weight_levels, axis=0)
    far_flat = far_nodes.reshape(-1)
    far_points = jnp.take(tree_points, far_flat, axis=0).reshape(LEAF_DEV, FAR, RANK, D)
    far_weights = jnp.take(tree_weights, far_flat, axis=0).reshape(LEAF_DEV, FAR, RANK, NRHS)
    leaf_terms = lax.map(
        leaf_image, (own_points, near_points, near_values, far_points, far_weights)
    )
    matvec_image = LAMBDA_RIDGE * residual + leaf_terms.reshape(points.shape[0], NRHS)
    gram_matrix, cross_product = lax.psum(
        (
            jnp.dot(matvec_image.T, matvec_image, precision=FULL_PRECISION),
            jnp.dot(matvec_image.T, residual, precision=FULL_PRECISION),
        ),
        ("gx", "gy"),
    )
    step_coeffs = cholesky_solve(gram_matrix, cross_product)
    solution_next = solution + jnp.dot(residual, step_coeffs, precision=FULL_PRECISION)
    residual_next = residual - jnp.dot(matvec_image, step_coeffs, precision=FULL_PRECISION)
    return (solution_next, residual_next, matvec_image)


def solution(mesh):
    placed = (
        P(("gx", "gy"), None),
        P(("gx", "gy"), None),
        P(("gx", "gy"), None),
        P(("gx", "gy"), None),
        P(("gx", "gy"), None),
        P(),
        P(("gx", "gy"), None),
    )
    return jax.shard_map(
        shards,
        mesh=mesh,
        in_specs=placed,
        out_specs=(P(("gx", "gy"), None), P(("gx", "gy"), None), P(("gx", "gy"), None)),
        check_vma=False,
    )
```

profile of v0, /device:TPU:0, one launch (start us, length us, event | category | flops | bytes accessed | tf_op | source)
XLA Modules:
  0.0 403.2 jit_solution(9086683935424094712)
XLA Ops:
  7.2 1.1 copy.103
  8.3 0.9 reshape.473
  13.6 32.8 %all_gather.20 = bf16[8,128,64]{1,2,0:T(8,128)(2,1)S(1)} all-gather(bf16[1,128,64]{1,2,0:T(8,128)(2,1)S(1)} %copy.109), channel_id=1, replica_groups=mesh['gx'=4,'gy'=8] {'gy'}, dimensions={0}, use_global_device_ids=true | all-gather | bytes 147456 | tf_op jit(solution)/shard_map/all_gather | solution.py:179
  46.8 1.0 multiply_reduce_fusion.3
  47.8 0.8 fusion.150
  48.6 0.8 compare_and_fusion
  49.4 3.2 gather_fusion.3
  52.9 1.7 gather_fusion.4
  55.6 1.0 gather_fusion.5
  56.9 9.5 %all_gather.21 = bf16[60,128,64]{1,2,0:T(8,128)(2,1)S(1)} all-gather(bf16[15,128,64]{1,2,0:T(8,128)(2,1)S(1)} %pad_maximum_fusion.2), channel_id=1, replica_groups=mesh['gx'=4,'gy'=8] {'gx'}, dimensions={0}, use_global_device_ids=true | all-gather | bytes 1228800 | tf_op jit(solution)/shard_map/all_gather | solution.py:184
  68.0 30.5 %all-gather = f32[1024,32]{0,1:T(8,128)S(1)} all-gather(f32[128,32]{0,1:T(8,128)S(1)} %convolution_multiply_fusion.6), channel_id=2, replica_groups=mesh['gx'=4,'gy'=8] {'gy'}, dimensions={0}, use_global_device_ids=true | all-gather | bytes 147456 | tf_op jit(solution)/shard_map/all_gather | solution.py:180
  100.6 6.4 %all_gather.23 = bf16[60,128,32]{1,2,0:T(8,128)(2,1)S(1)} all-gather(bf16[15,128,32]{1,2,0:T(8,128)(2,1)S(1)} %pad_maximum_fusion.3), channel_id=1, replica_groups=mesh['gx'=4,'gy'=8] {'gx'}, dimensions={0}, use_global_device_ids=true | all-gather | bytes 614400 | tf_op jit(solution)/shard_map/all_gather | solution.py:185
  108.5 0.9 slice.63
  110.7 1.7 gather_fusion.6
  112.7 1.0 gather_fusion.7
  115.1 0.9 copy.137
  116.0 1.0 copy.138
  117.0 1.1 copy.139
  118.8 1.4 copy_dynamic-update-slice_fusion.1
  120.2 1.5 copy_dynamic-update-slice_fusion
  121.7 1.6 constant_dynamic-update-slice_fusion.2
  125.0 0.9 constant_dynamic-update-slice_fusion
  125.8 1.9 gather_fusion.1
  128.1 31.5 %all-gather.2 = bf16[8,2,16384]{2,1,0:T(2,128)(2,1)S(1)} all-gather(bf16[1,2,16384]{2,1,0:T(2,128)(2,1)S(1)} %reshape.475), channel_id=1, replica_groups=mesh['gx'=4,'gy'=8] {'gy'}, dimensions={0}, use_global_device_ids=true | all-gather | bytes 589824 | tf_op jit(solution)/shard_map/all_gather | solution.py:155
  160.1 0.8 reshape.371
  161.3 0.9 broadcast_select_fusion.1
  162.4 1.5 reshape.474
  164.2 2.1 reshape.368
  166.3 1.5 pad_maximum_fusion
  168.4 16.0 %while.53 = (s32[]{:T(128)}, f32[2,512,32]{1,0,2:T(2,128)}, bf16[2,512,64]{1,2,0:T(8,128)(2,1)S(1)}, bf16[2,5,512,64]{2,3,1,0:T(8,128)(2,1)S(1)}, bf16[2,5,512,3...) while((s32[]{:T(128)}, f32[2,512,32]{1,0,2:T(2,128)}, ...), condition=%wide.region_18.21_spmd, body=%wide.region_14.20_spmd.sunk | while | flops 800304128 | bytes 13847237 | solution.py:200
  169.5 3.5 fusion.244
  173.2 1.9 fusion.245
  177.5 3.5 fusion.244
  181.1 1.9 fusion.245
  184.4 0.9 copy.174
  185.9 39.4 %all-reduce = (f32[32,32]{1,0:T(8,128)S(1)}, f32[32,32]{1,0:T(8,128)S(1)}) all-reduce(f32[32,32]{1,0:T(8,128)S(1)} %fusion.163, f32[32,32]{1,0:T(8,128)S(1)} %fusion.164), channel_id=1, replica_groups=mesh['gx'=4,'gy'=8] {'gx','gy'}, use_global_device_ids=true, to_apply=%region_23.26 | all-reduce | flops 2048 | bytes 16384 | tf_op jit(solution)/shard_map/psum | solution.py:204
  225.2 58.2 %while.56 = (s32[]{:T(128)}, f32[32,32]{1,0:T(8,128)S(1)}, f32[32,32]{1,0:T(8,128)S(1)}, s32[]{:T(128)}, s32[]{:T(128)}) while((s32[]{:T(128)}, f32[32,32]{1,0:T(8,128)S(1)}, f32[32,32]{1,0:T(8,128)S(1)}, s32[]{:T(128)}, s32[]{:T(128)}) %tuple.134), condition=%wide.region_22.25_spmd.clone.clone, body=%wide.region_20.24_spmd.clone.clone.sunk | while | flops 42338 | bytes 21869 | solution.py:62
  225.5 0.8 fusion.270
  227.3 0.8 fusion.270
  229.1 0.8 fusion.270
  231.0 0.8 fusion.270
  232.8 0.8 fusion.270
  238.2 0.8 fusion.270
  272.8 0.8 fusion.270
  283.6 55.3 %while.54 = (s32[]{:T(128)}, f32[32,32]{1,0:T(8,128)S(1)}, f32[32,32]{1,0:T(8,128)S(1)}, f32[32,32]{1,0:T(8,128)S(1)}, f32[32]{0:T(128)S(1)}, /*index=5*/s32[]{:T(128)}, s32[]{:T(128)}) while((s32[]{:T(128)}, f32[32,32]{1,0:T(8,128)S(1)}, f32[32,32]{1,0:T(8,128)S(1)}, f32[32,32]{1,0:T(8,128)S(1)}, f32[32]{0:T(128)S(1)}, ...), condition=%wide.region_27.30_spmd.clone, body=%wide.region_25.29_spmd.clone.sunk | while | flops 41250 | bytes 21744 | solution.py:74
  338.9 55.6 %while.55 = (s32[]{:T(128)}, f32[32,32]{1,0:T(8,128)S(1)}, f32[32,32]{1,0:T(8,128)S(1)}, f32[32,32]{1,0:T(8,128)S(1)}, f32[32]{0:T(128)S(1)}, /*index=5*/s32[]{:T(128)}, s32[]{:T(128)}, s32[]{:T(128)}) while((s32[]{:T(128)}, f32[32,32]{1,0:T(8,128)S(1)}, f32[32,32]{1,0:T(8,128)S(1)}, f32[32,32]{1,0:T(8,128)S(1)}, ...), condition=%wide.region_30.33_spmd.clone, body=%wide.region_28.32_spmd.clone.sunk | while | flops 41251 | bytes 21764 | solution.py:86
  394.4 1.0 convolution_subtract_fusion
  395.4 1.0 fusion.120
  (712 shorter events, 165.5 us)
Async XLA Ops:
  7.2 155.2 %all-gather.5.cloned.1.call-start = ((), (), s32[]{:S(2)}) async-start(), calls=%async_computation | async-start | bytes 1179648 | tf_op jit(solution)/shard_map/all_gather | solution.py:154
  8.3 58.8 %copy-start.2 = (bf16[1024,64]{0,1:T(8,128)(2,1)S(1)}, bf16[1024,64]{0,1:T(8,128)(2,1)}, u32[]{:S(2)}) copy-start(bf16[1024,64]{0,1:T(8,128)(2,1)} %param.19) | copy-start | bytes 393220
  13.4 54.0 %copy-start = (f32[1024,32]{0,1:T(8,128)S(1)}, f32[1024,32]{0,1:T(8,128)}, u32[]{:S(2)}) copy-start(f32[1024,32]{0,1:T(8,128)} %param.21) | copy-start | bytes 393220
  107.0 11.1 %copy-start.11 = (s32[2,16]{1,0:T(2,128)S(1)}, s32[2,16]{1,0:T(2,128)}, u32[]{:S(2)}) copy-start(s32[2,16]{1,0:T(2,128)} %param.25) | copy-start | bytes 388
  112.6 2.2 copy-start.6
  123.4 4.3 %copy-start.10 = (s32[2,4]{1,0:T(2,128)S(1)}, s32[2,4]{1,0:T(2,128)}, u32[]{:S(2)}) copy-start(s32[2,4]{1,0:T(2,128)} %param.22) | copy-start | bytes 100
  125.0 36.2 %copy-start.3 = (bf16[1024,64]{0,1:T(8,128)(2,1)S(1)}, bf16[1024,64]{0,1:T(8,128)(2,1)}, u32[]{:S(2)}) copy-start(bf16[1024,64]{0,1:T(8,128)(2,1)} %param.19) | copy-start | bytes 393220
  168.4 170.5 %copy-start.4 = (f32[32,32]{1,0:T(8,128)S(1)}, f32[32,32]{1,0:T(8,128)}, u32[]{:S(2)}) copy-start(f32[32,32]{1,0:T(8,128)} %custom-call.11) | copy-start | bytes 12292
  168.4 227.0 %copy-start.7 = (f32[1024,32]{0,1:T(8,128)S(1)}, f32[1024,32]{0,1:T(8,128)}, u32[]{:S(2)}) copy-start(f32[1024,32]{0,1:T(8,128)} %param.20) | copy-start | bytes 393220
  168.4 1.1 copy-start.5
  173.1 2.1 copy-start.8
  175.8 0.7 copy-start.9
  176.4 1.0 copy-start.5
  181.0 2.1 copy-start.8
  183.7 0.7 copy-start.9
  185.3 211.0 %copy-start.1 = (f32[1024,32]{0,1:T(8,128)}, f32[1024,32]{0,1:T(8,128)S(1)}, u32[]{:S(2)}) copy-start(f32[1024,32]{0,1:T(8,128)S(1)} %add.319) | copy-start | bytes 393220
Sparse Core Ops, SparseCore 0:
  10.7 43.5 all-gather.4
where the time goes:
time: 405 us; the launch traced here: 403 us
  blocking collectives  150 us (37%)
  matrix products  118 us (29%)
  other arithmetic  58.9 us (15%)
  local copies, waits for them, and re-layouts  38.4 us (9%)
  loops' own time  23.1 us (6%)
  between operations  14.7 us (4%)
    psum x1, blocking collectives, shards(): lax.psum((jnp.dot(matvec_image.T, matvec_image, precision=FULL_PRECISION)...  39.4 us
    all_gather x1, blocking collectives, shards(): row_points = lax.all_gather(skeleton_points[None], 'gy', axis=0, tiled=True)  32.8 us
    all_gather x1, blocking collectives, shards(): piece_values = lax.all_gather(flat_values, 'gy', axis=0, tiled=True)  31.5 us
    all_gather x1, blocking collectives, shards(): row_weights = lax.all_gather(node_weights[None], 'gy', axis=0, tiled=True)  30.5 us
    dot_general x32, matrix products, factor_step(): jnp.dot(lower, lower_row, precision=FULL_PRECISION)  24.9 us
    dot_general x32, matrix products, forward_step(): jnp.dot(lower_row, partial_value, precision=FULL_PRECISION)  24.7 us
    dot_general x32, matrix products, backward_step(): jnp.dot(lower_column, partial_value, precision=FULL_PRECISION)  24.7 us
    another operation x1, loops' own time, cholesky_solve(): lower = lax.fori_loop(0, order, factor_step, jnp.zeros_like(matrix))  22.7 us
  transfers between devices with their start and end apart: 1, of which 0 were waited for; matrix products, arithmetic and copies ran while one was open for 10% of the time, Pallas kernels for 0%

commit v1 on v0

--- a/solution.py
+++ b/solution.py
@@ -143,6 +143,12 @@
 
 
 def shards(points, solution, residual, near_leaves, node_skeleton, upper_skeleton, far_nodes):
+
+    def attach_runs(z_in, page):
+        m_next = jnp.concatenate([z_in, page], 1)
+        mid_arr = lax.all_gather(m_next, "gy", axis=0, tiled=True)
+        return jnp.split(mid_arr, [z_in.shape[1]], axis=1)
+
     gx_count = lax.axis_size("gx")
     gy_count = lax.axis_size("gy")
     row_index = lax.axis_index("gx")
@@ -151,8 +157,7 @@
     flat_values = values_half.reshape(LEAF_DEV, LEAF * NRHS)
     request_total = LEAF_DEV * NEAR
     wanted_leaves = near_leaves.reshape(request_total) - row_index * (gy_count * LEAF_DEV)
-    piece_points = lax.all_gather(flat_points, "gy", axis=0, tiled=True)
-    piece_values = lax.all_gather(flat_values, "gy", axis=0, tiled=True)
+    piece_points, piece_values = attach_runs(flat_points, flat_values)
     positions = jnp.arange(piece_points.shape[0], dtype=jnp.int32)
     onehot = (wanted_leaves[:, None] == positions[None, :]).astype(jnp.bfloat16)
     got_points = jnp.dot(onehot, piece_points, preferred_element_type=jnp.float32)

time: 405 us -> 375 us (0.926)
  blocking collectives: 150 us -> 119 us
  other arithmetic: 58.9 us -> 63 us
    all_gather x1 -> x0, blocking collectives: 31.5 us -> none  [shards(): piece_values = lax.all_gather(flat_values, 'gy', axis=0, tiled=True)]
    unnamed x34 -> x37, local copies, waits for them, and re-layouts: 11.4 us -> 6.1 us
  transfers between devices with their start and end apart: 1 -> 1, of which waited for: 0 -> 0; matrix products, arithmetic and copies ran while one was open for 10% -> 11% of each run, Pallas kernels for 0% -> 0%
where the time goes in v1:
time: 375 us; the launch traced here: 373 us
  blocking collectives  119 us (32%)
  matrix products  118 us (31%)
  other arithmetic  63 us (17%)
  local copies, waits for them, and re-layouts  36.2 us (10%)
  loops' own time  23.1 us (6%)
  between operations  14.6 us (4%)
    psum x1, blocking collectives, shards(): lax.psum((jnp.dot(matvec_image.T, matvec_image, precision=FULL_PRECISION)...  39.3 us
    all_gather x1, blocking collectives, shards(): row_points = lax.all_gather(skeleton_points[None], 'gy', axis=0, tiled=True)  32.7 us
    all_gather x1, blocking collectives, shards(): row_weights = lax.all_gather(node_weights[None], 'gy', axis=0, tiled=True)  30.5 us
    dot_general x32, matrix products, factor_step(): jnp.dot(lower, lower_row, precision=FULL_PRECISION)  24.9 us
    dot_general x32, matrix products, forward_step(): jnp.dot(lower_row, partial_value, precision=FULL_PRECISION)  24.7 us
    dot_general x32, matrix products, backward_step(): jnp.dot(lower_column, partial_value, precision=FULL_PRECISION)  24.7 us
    another operation x1, loops' own time, cholesky_solve(): lower = lax.fori_loop(0, order, factor_step, jnp.zeros_like(matrix))  22.7 us
    reduce_sum x32, other arithmetic, backward_step(): jnp.sum(diagonal_part * pick)  20.2 us
  transfers between devices with their start and end apart: 1, of which 0 were waited for; matrix products, arithmetic and copies ran while one was open for 11% of the time, Pallas kernels for 0%

profile of v1, /device:TPU:0, one launch (start us, length us, event | category | flops | bytes accessed | tf_op | source)
XLA Modules:
  0.0 373.3 jit_solution(5710513791303452102)
XLA Ops:
  7.2 1.1 copy.103
  8.5 0.9 convert_element_type.98
  10.0 0.9 maximum_bitcast_fusion
  15.2 32.7 %all_gather.16 = bf16[8,128,64]{1,2,0:T(8,128)(2,1)S(1)} all-gather(bf16[1,128,64]{1,2,0:T(8,128)(2,1)S(1)} %copy.109), channel_id=1, replica_groups=mesh['gx'=4,'gy'=8] {'gy'}, dimensions={0}, use_global_device_ids=true | all-gather | bytes 147456 | tf_op jit(solution)/shard_map/all_gather | solution.py:184
  48.3 1.0 multiply_reduce_fusion.3
  49.3 0.8 fusion.152
  50.0 1.3 compare_and_fusion
  51.4 3.2 gather_fusion.3
  54.9 1.7 gather_fusion.4
  56.8 1.3 and_bitcast_fusion.1
  58.1 1.0 gather_fusion.5
  59.4 9.6 %all_gather.17 = bf16[60,128,64]{1,2,0:T(8,128)(2,1)S(1)} all-gather(bf16[15,128,64]{1,2,0:T(8,128)(2,1)S(1)} %pad_maximum_fusion.2), channel_id=1, replica_groups=mesh['gx'=4,'gy'=8] {'gx'}, dimensions={0}, use_global_device_ids=true | all-gather | bytes 1228800 | tf_op jit(solution)/shard_map/all_gather | solution.py:189
  71.1 30.5 %all-gather = f32[1024,32]{0,1:T(8,128)S(1)} all-gather(f32[128,32]{0,1:T(8,128)S(1)} %convolution_multiply_fusion.6), channel_id=2, replica_groups=mesh['gx'=4,'gy'=8] {'gy'}, dimensions={0}, use_global_device_ids=true | all-gather | bytes 147456 | tf_op jit(solution)/shard_map/all_gather | solution.py:185
  103.7 6.4 %all_gather.19 = bf16[60,128,32]{1,2,0:T(8,128)(2,1)S(1)} all-gather(bf16[15,128,32]{1,2,0:T(8,128)(2,1)S(1)} %pad_maximum_fusion.3), channel_id=1, replica_groups=mesh['gx'=4,'gy'=8] {'gx'}, dimensions={0}, use_global_device_ids=true | all-gather | bytes 614400 | tf_op jit(solution)/shard_map/all_gather | solution.py:190
  111.6 0.8 slice.63
  114.7 1.7 gather_fusion.6
  117.9 1.6 copy.137
  119.5 1.7 copy.138
  121.2 1.9 copy.139
  123.2 1.0 gather_fusion.7
  126.1 0.9 constant_dynamic-update-slice_fusion.6
  127.0 1.0 constant_dynamic-update-slice_fusion.5
  128.0 1.1 constant_dynamic-update-slice_fusion.4
  129.8 1.0 constant_dynamic-update-slice_fusion.1
  131.7 0.9 broadcast_select_fusion.1
  132.8 1.9 reshape.474
  135.4 2.1 reshape.369
  137.5 1.5 pad_maximum_fusion
  139.6 0.8 reshape.371
  140.8 14.6 %while.53 = (s32[]{:T(128)}, f32[2,512,32]{1,0,2:T(2,128)S(1)}, bf16[2,512,64]{1,2,0:T(8,128)(2,1)S(1)}, bf16[2,5,512,64]{2,3,1,0:T(8,128)(2,1)S(1)}, bf16[2,5,5...) while((s32[]{:T(128)}, f32[2,512,32]{1,0,2:T(2,128)S(1)}, ...), condition=%wide.region_18.21_spmd, body=%wide.region_14.20_spmd.sunk | while | flops 800304128 | bytes 12798605 | solution.py:205
  141.9 3.5 fusion.244
  145.5 1.9 fusion.245
  149.2 3.5 fusion.244
  152.8 1.9 fusion.245
  156.0 39.3 %all-reduce = (f32[32,32]{1,0:T(8,128)S(1)}, f32[32,32]{1,0:T(8,128)S(1)}) all-reduce(f32[32,32]{1,0:T(8,128)S(1)} %fusion.165, f32[32,32]{1,0:T(8,128)S(1)} %fusion.166), channel_id=1, replica_groups=mesh['gx'=4,'gy'=8] {'gx','gy'}, use_global_device_ids=true, to_apply=%region_23.26 | all-reduce | flops 2048 | bytes 16384 | tf_op jit(solution)/shard_map/psum | solution.py:209
  195.3 58.2 %while.56 = (s32[]{:T(128)}, f32[32,32]{1,0:T(8,128)S(1)}, f32[32,32]{1,0:T(8,128)S(1)}, s32[]{:T(128)}, s32[]{:T(128)}) while((s32[]{:T(128)}, f32[32,32]{1,0:T(8,128)S(1)}, f32[32,32]{1,0:T(8,128)S(1)}, s32[]{:T(128)}, s32[]{:T(128)}) %tuple.134), condition=%wide.region_22.25_spmd.clone.clone, body=%wide.region_20.24_spmd.clone.clone.sunk | while | flops 42338 | bytes 21869 | solution.py:62
  195.6 0.8 fusion.270
  197.4 0.8 fusion.270
  199.2 0.8 fusion.270
  201.1 0.8 fusion.270
  202.9 0.8 fusion.270
  204.7 0.8 fusion.270
  212.0 0.8 fusion.270
  246.5 0.8 fusion.270
  253.7 55.2 %while.54 = (s32[]{:T(128)}, f32[32,32]{1,0:T(8,128)S(1)}, f32[32,32]{1,0:T(8,128)S(1)}, f32[32,32]{1,0:T(8,128)S(1)}, f32[32]{0:T(128)S(1)}, /*index=5*/s32[]{:T(128)}, s32[]{:T(128)}) while((s32[]{:T(128)}, f32[32,32]{1,0:T(8,128)S(1)}, f32[32,32]{1,0:T(8,128)S(1)}, f32[32,32]{1,0:T(8,128)S(1)}, f32[32]{0:T(128)S(1)}, ...), condition=%wide.region_27.30_spmd.clone, body=%wide.region_25.29_spmd.clone.sunk | while | flops 41250 | bytes 21744 | solution.py:74
  308.9 55.6 %while.55 = (s32[]{:T(128)}, f32[32,32]{1,0:T(8,128)S(1)}, f32[32,32]{1,0:T(8,128)S(1)}, f32[32,32]{1,0:T(8,128)S(1)}, f32[32]{0:T(128)S(1)}, /*index=5*/s32[]{:T(128)}, s32[]{:T(128)}, s32[]{:T(128)}) while((s32[]{:T(128)}, f32[32,32]{1,0:T(8,128)S(1)}, f32[32,32]{1,0:T(8,128)S(1)}, f32[32,32]{1,0:T(8,128)S(1)}, ...), condition=%wide.region_30.33_spmd.clone, body=%wide.region_28.32_spmd.clone.sunk | while | flops 41251 | bytes 21764 | solution.py:86
  364.5 1.0 convolution_subtract_fusion
  365.5 1.0 fusion.120
  (709 shorter events, 165.2 us)
Async XLA Ops:
  7.2 125.6 %all-gather.4.cloned.1.call-start = ((), (), s32[]{:S(2)}) async-start(), calls=%async_computation | async-start | bytes 1769472 | tf_op jit(solution)/shard_map/all_gather | solution.py:149
  9.9 60.2 %copy-start.2 = (bf16[1024,64]{0,1:T(8,128)(2,1)S(1)}, bf16[1024,64]{0,1:T(8,128)(2,1)}, u32[]{:S(2)}) copy-start(bf16[1024,64]{0,1:T(8,128)(2,1)} %param.19) | copy-start | bytes 393220
  15.0 55.5 %copy-start = (f32[1024,32]{0,1:T(8,128)S(1)}, f32[1024,32]{0,1:T(8,128)}, u32[]{:S(2)}) copy-start(f32[1024,32]{0,1:T(8,128)} %param.21) | copy-start | bytes 393220
  110.1 13.0 %copy-start.11 = (s32[2,16]{1,0:T(2,128)S(1)}, s32[2,16]{1,0:T(2,128)}, u32[]{:S(2)}) copy-start(s32[2,16]{1,0:T(2,128)} %param.25) | copy-start | bytes 388
  110.1 14.0 %copy-start.9 = (pred[128]{0:T(512)(128)(4,1)S(1)}, pred[128]{0:T(512)(128)(4,1)}, u32[]{:S(2)}) copy-start(pred[128]{0:T(512)(128)(4,1)} %get-tuple-element.489) | copy-start | bytes 388
  123.1 6.7 %copy-start.3 = (bf16[4,2,128,64]{2,3,1,0:T(8,128)(2,1)S(1)}, bf16[4,2,128,64]{2,3,1,0:T(8,128)(2,1)}, u32[]{:S(2)}) copy-start(bf16[4,2,128,64]{2,3,1,0:T(8,128)(2,1)} %slice.56) | copy-start | bytes 393220
  125.3 4.4 %copy-start.8 = (bf16[1,128,64]{1,2,0:T(8,128)(2,1)S(1)}, bf16[1,128,64]{1,2,0:T(8,128)(2,1)}, u32[]{:S(2)}) copy-start(bf16[1,128,64]{1,2,0:T(8,128)(2,1)} %copy.120) | copy-start | bytes 49156
  129.1 2.5 copy-start.10
  129.1 2.6 copy-start.5
  129.1 2.6 copy-start.12
  137.5 3.3 copy-start.7
  140.8 224.7 %copy-start.6 = (f32[1024,32]{0,1:T(8,128)S(1)}, f32[1024,32]{0,1:T(8,128)}, u32[]{:S(2)}) copy-start(f32[1024,32]{0,1:T(8,128)} %param.20) | copy-start | bytes 393220
  140.8 1.1 copy-start.4
  148.1 1.0 copy-start.4
  155.5 211.0 %copy-start.1 = (f32[1024,32]{0,1:T(8,128)}, f32[1024,32]{0,1:T(8,128)S(1)}, u32[]{:S(2)}) copy-start(f32[1024,32]{0,1:T(8,128)S(1)} %add.319) | copy-start | bytes 393220
Sparse Core Ops, SparseCore 0:
  11.0 47.4 all-gather.3
